TPU v7x, 32 devices: a whole 2x2x4 slice. The times are simulated.
32 devices in a mesh: sp: 4 (over y, x), fsdp: 8 (over z, core).
Axes of the slice: x: 2, y: 2, z: 4, core: 2. Of those that a mesh axis runs over, the one named last changes fastest.
Arguments:
- layer_input: bfloat16 [8, 1024, 2048], P('fsdp', 'sp'), may hold values from -6 to 6
- positions: int32 [8, 1024], P('fsdp'), may hold values from 0 to 1023, as said below
- cotangent: bfloat16 [8, 1024, 2048], P('fsdp', 'sp'), may hold values from -6 to 6
- w_qkv: bfloat16 [2048, 1536], P('fsdp'), may hold values from -0.125 to 0.125
- w_out: bfloat16 [1024, 2048], P('fsdp'), may hold values from -1 to 1
- w_gate: bfloat16 [2048, 4096], P('fsdp'), may hold values from -0.125 to 0.125
- w_up: bfloat16 [2048, 4096], P('fsdp'), may hold values from -0.125 to 0.125
- w_down: bfloat16 [4096, 2048], P('fsdp'), may hold values from -0.09375 to 0.09375
- gain_attn: bfloat16 [2048], P('fsdp'), may hold values from 0.099609375 to 1.8984375
- gain_ffn: bfloat16 [2048], P('fsdp'), may hold values from 0.099609375 to 1.8984375
- gain_query: bfloat16 [64], replicated, may hold values from 1 to 2
- gain_key: bfloat16 [64], replicated, may hold values from 1 to 2
Outputs:
- out: bfloat16 [8, 1024, 2048], P('fsdp', 'sp')
- grad_input: float32 [8, 1024, 2048], P('fsdp', 'sp')
- grad_qkv: float32 [2048, 1536], P(('sp', 'fsdp'))
- grad_out: float32 [1024, 2048], P(('sp', 'fsdp'))
- grad_gate: float32 [2048, 4096], P(('sp', 'fsdp'))
- grad_up: float32 [2048, 4096], P(('sp', 'fsdp'))
- grad_down: float32 [4096, 2048], P(('sp', 'fsdp'))
- grad_gain_attn: float32 [2048], P(('sp', 'fsdp'))
- grad_gain_ffn: float32 [2048], P(('sp', 'fsdp'))
- grad_gain_query: float32 [64], replicated
- grad_gain_key: float32 [64], replicated
Inputs may be any that keep to these rules, and one draw needn't show every extreme that they name: `positions`: in each sequence the first position is 0, and every later position is either 0 (a new document starts) or the previous position plus 1. The first sequence is a single document.
All inputs are finite; a program needn't handle non-finite values.
Results may differ from a plain program's by a relative error of at most 0.015.
The roundings to bfloat16 on the way count: a program that leaves them out, or rounds other values in their place, can miss the bound.
Values may be sent and summed in bfloat16 or wider, within the bound.
A program may use at most 320 MiB of HBM per device.

v0:
```python
import jax
import jax.numpy as jnp
from jax import lax
from jax.sharding import PartitionSpec as P

QUERY_HEADS = 16
KV_HEADS = 4
HD = 64
EPS = 1e-06
f32 = jnp.float32
bf16 = jnp.bfloat16


def rms_scale(values, gain):
    return values * lax.rsqrt(jnp.mean(values * values, axis=-1, keepdims=True) + EPS) * gain


def rope_tables(position_ids):
    half = HD // 2
    frequency = 10000.0 ** (-2.0 * jnp.arange(half, dtype=f32) / HD)
    angles = position_ids.astype(f32)[:, None, None] * frequency
    return (jnp.cos(angles), jnp.sin(angles))


def rotate(values, cosine, sine):
    half = HD // 2
    front, back = (values[..., :half], values[..., half:])
    return jnp.concatenate([front * cosine - back * sine, back * cosine + front * sine], axis=-1)


def over_rows(a, b):
    return lax.dot_general(a, b, (((0,), (0,)), ((), ())), preferred_element_type=f32)


def times_transposed(a, b):
    return lax.dot_general(a, b, (((1,), (1,)), ((), ())), preferred_element_type=f32)


def masked_scores(q, k, position_ids):
    length = q.shape[0]
    scores = jnp.einsum("qgd,td->gqt", q, k, preferred_element_type=f32) * HD ** (-0.5)
    qi = jnp.arange(length, dtype=jnp.int32)[:, None]
    ki = jnp.arange(length, dtype=jnp.int32)[None, :]
    allowed = (ki <= qi) & (qi - ki <= position_ids[:, None])
    return (jnp.where(allowed, scores, -1e30), allowed)


def attend(q, k, v, position_ids):
    masked, _ = masked_scores(q, k, position_ids)
    largest = jnp.max(masked, axis=-1, keepdims=True)
    exponent = jnp.exp(masked - largest)
    total = jnp.sum(exponent, axis=-1, keepdims=True)
    probs = (exponent / total).astype(bf16)
    mixture = jnp.einsum("gqt,td->qgd", probs, v, preferred_element_type=f32)
    return (mixture.astype(bf16), (largest + jnp.log(total))[..., 0])


def attend_back(q, k, v, position_ids, grad_mixture, log_total):
    masked, allowed = masked_scores(q, k, position_ids)
    probs = jnp.exp(masked - log_total[..., None])
    grad_v = jnp.einsum("gqt,qgd->td", probs.astype(bf16), grad_mixture, preferred_element_type=f32)
    grad_p = jnp.einsum("qgd,td->gqt", grad_mixture, v, preferred_element_type=f32)
    inner = jnp.sum(grad_p * probs, axis=-1, keepdims=True)
    grad_s = jnp.where(allowed, probs * (grad_p - inner), 0.0).astype(bf16)
    scale = HD ** (-0.5)
    grad_q = jnp.einsum("gqt,td->qgd", grad_s, k, preferred_element_type=f32) * scale
    grad_k = jnp.einsum("gqt,qgd->td", grad_s, q, preferred_element_type=f32) * scale
    return (grad_q.astype(bf16), grad_k.astype(bf16), grad_v.astype(bf16))


def swap(value, mask, count):
    return lax.ppermute(value, "sp", [(i, i ^ mask) for i in range(count)])


def gather_chunks(chunk, s, count):
    if count != 4:
        return lax.all_gather(chunk, "sp", axis=0)
    half = chunk.shape[0] // 2
    over_x = swap(chunk, 1, count)
    over_y = swap(chunk, 2, count)
    first = swap(over_x[:half], 2, count)
    second = swap(over_y[half:], 1, count)
    stack = jnp.zeros((count,) + chunk.shape, chunk.dtype)
    for mask, part in ((0, chunk), (1, over_x), (2, over_y)):
        stack = lax.dynamic_update_slice_in_dim(stack, part[None], s ^ mask, 0)
    across = jnp.concatenate([first, second], axis=0)
    return lax.dynamic_update_slice_in_dim(stack, across[None], s ^ 3, 0)


def scatter_sum(partial, s, count):
    rows = partial.shape[0] // count
    if count != 4:
        return lax.psum_scatter(partial.astype(bf16), "sp", scatter_dimension=0, tiled=True).astype(
            f32
        )
    half = rows // 2

    def part(mask):
        return lax.dynamic_slice_in_dim(partial, (s ^ mask) * rows, rows, 0)

    across = part(3).astype(bf16)
    from_y = swap(across[:half], 2, count)
    from_x = swap(across[half:], 1, count)
    to_x, to_y = (part(1), part(2))
    to_x = jnp.concatenate([to_x[:half] + from_y.astype(f32), to_x[half:]], axis=0).astype(bf16)
    to_y = jnp.concatenate([to_y[:half], to_y[half:] + from_x.astype(f32)], axis=0).astype(bf16)
    return part(0) + swap(to_x, 1, count).astype(f32) + swap(to_y, 2, count).astype(f32)


def local(
    x_own,
    positions,
    ct_own,
    w_qkv,
    w_out,
    w_gate,
    w_up,
    w_down,
    gain_attn,
    gain_ffn,
    gain_query,
    gain_key,
):
    S, F = (lax.axis_size("sp"), lax.axis_size("fsdp"))
    s = lax.axis_index("sp")
    _, T, D = x_own.shape
    L = positions.shape[1]
    pos = positions[0]
    copies = max(1, S // KV_HEADS)
    QW = QUERY_HEADS * HD
    KW = KV_HEADS * HD
    heads = QUERY_HEADS // S
    qw = heads * HD
    FF = w_gate.shape[1]
    FFs = FF // S
    rows_d = D // (S * F)
    x_own = x_own[0]
    ct_own = ct_own[0]

    def cut(w, start, size, axis):
        return lax.dynamic_slice_in_dim(w, start, size, axis)

    def regroup(w):
        size = w.shape[0] // S
        perm = [(i * F + j, j * S + i) for i in range(S) for j in range(F)]
        return lax.ppermute(cut(w, s * size, size, 0), ("sp", "fsdp"), perm)

    def gather_z(w):
        return lax.all_gather(w, "fsdp", axis=0, tiled=True)

    gains = jnp.pad(jnp.stack([gain_attn, gain_ffn], axis=1), ((0, 0), (0, 126)))
    kv = s // copies
    attn_part = jnp.concatenate(
        [
            cut(w_qkv, s * qw, qw, 1),
            cut(w_qkv, QW + kv * HD, HD, 1),
            cut(w_qkv, QW + KW + kv * HD, HD, 1),
            gains,
        ],
        axis=1,
    )
    attn_full = gather_z(attn_part)
    hw = qw + 2 * HD
    wqkv_s = attn_full[:, :hw]
    g_attn = attn_full[:, hw].astype(f32)
    g_ffn = attn_full[:, hw + 1].astype(f32)
    wout_s = gather_z(regroup(w_out))
    gu_part = jnp.concatenate([cut(w_gate, s * FFs, FFs, 1), cut(w_up, s * FFs, FFs, 1)], axis=1)
    w_gu = gather_z(gu_part)
    w_dn = gather_z(regroup(w_down))
    x_bf = gather_chunks(x_own, s, S).reshape(L, D)
    x_all = x_bf.astype(f32)
    normed = rms_scale(x_all, g_attn).astype(bf16)
    projected = jnp.dot(normed, wqkv_s, preferred_element_type=f32)
    cosine, sine = rope_tables(pos)

    def prep(raw, gain):
        return rotate(rms_scale(raw, gain), cosine, sine)

    q_rot, q_pull = jax.vjp(prep, projected[:, :qw].reshape(L, heads, HD), gain_query.astype(f32))
    k_rot, k_pull = jax.vjp(
        prep, projected[:, qw : qw + HD].reshape(L, 1, HD), gain_key.astype(f32)
    )
    q = q_rot.astype(bf16)
    k = k_rot.astype(bf16)[:, 0]
    v = projected[:, qw + HD :].astype(bf16)
    mixture, log_total = attend(q, k, v, pos)
    mix_s = mixture.reshape(L, qw)
    mix_all = jnp.swapaxes(gather_chunks(mix_s, s, S), 0, 1).reshape(L, QW)
    wout_full = gather_chunks(wout_s, s, S).reshape(QW, D)
    middle = x_all + jnp.dot(mix_all, wout_full, preferred_element_type=f32)
    ffn_in = rms_scale(middle, g_ffn).astype(bf16)
    gu = jnp.dot(ffn_in, w_gu, preferred_element_type=f32)

    def gated(g, u):
        return jax.nn.silu(g) * u

    hidden_val, hidden_pull = jax.vjp(gated, gu[:, :FFs], gu[:, FFs:])
    hidden = hidden_val.astype(bf16)
    ct_all = gather_chunks(ct_own, s, S).reshape(L, D)
    grad_down = over_rows(hidden, ct_all).astype(bf16)
    grad_down = lax.psum_scatter(grad_down, "fsdp", scatter_dimension=0, tiled=True).astype(f32)
    grad_hidden = times_transposed(ct_all, w_dn)
    d_gate, d_up = hidden_pull(grad_hidden)
    d_gu = jnp.concatenate([d_gate.astype(bf16), d_up.astype(bf16)], axis=1)

    def share_rows(grad):
        width = grad.shape[1]
        grad = grad.astype(bf16).reshape(S, F, rows_d, width)
        grad = jnp.swapaxes(grad, 0, 1).reshape(D, width)
        mine = lax.psum_scatter(grad, "fsdp", scatter_dimension=0, tiled=True)
        mine = mine.reshape(S, rows_d, width)
        return lax.all_to_all(mine, "sp", split_axis=0, concat_axis=0)

    grad_gu = share_rows(over_rows(ffn_in, d_gu))
    grad_gate = jnp.swapaxes(grad_gu[:, :, :FFs], 0, 1).reshape(rows_d, FF).astype(f32)
    grad_up = jnp.swapaxes(grad_gu[:, :, FFs:], 0, 1).reshape(rows_d, FF).astype(f32)
    grad_ffn_in = scatter_sum(times_transposed(d_gu, w_gu), s, S)
    out_sum = scatter_sum(jnp.dot(hidden, w_dn, preferred_element_type=f32), s, S)
    middle_own = cut(middle, s * T, T, 0)
    out = (middle_own + out_sum).astype(bf16)
    _, ffn_pull = jax.vjp(rms_scale, middle_own, g_ffn)
    grad_middle, grad_g_ffn = ffn_pull(grad_ffn_in)
    grad_middle = ct_own.astype(f32) + grad_middle
    d_attn = grad_middle.astype(bf16)
    d_mix_tok = times_transposed(d_attn, wout_full).astype(bf16).reshape(T, S, qw)
    d_mix = lax.all_to_all(jnp.swapaxes(d_mix_tok, 0, 1), "sp", split_axis=0, concat_axis=0)
    d_mix = d_mix.reshape(L, heads, HD)
    d_attn_all = gather_chunks(d_attn, s, S).reshape(L, D)
    grad_out = over_rows(mix_s, d_attn_all).astype(bf16)
    grad_out = lax.psum_scatter(grad_out, "fsdp", scatter_dimension=0, tiled=True).astype(f32)
    dq, dk, dv = attend_back(q, k, v, pos, d_mix, log_total)
    dk, dv = (dk.astype(f32), dv.astype(f32))
    if copies > 1:
        groups = [[i * copies + j for j in range(copies)] for i in range(KV_HEADS)]
        dk, dv = lax.psum((dk, dv), "sp", axis_index_groups=groups)
        first = (s % copies == 0).astype(f32)
        dk, dv = (dk * first, dv * first)
    d_q_raw, grad_g_query = q_pull(dq.astype(f32))
    d_k_raw, grad_g_key = k_pull(dk[:, None])
    d_proj = jnp.concatenate([d_q_raw.reshape(L, qw), d_k_raw[:, 0], dv], axis=1).astype(bf16)
    grad_qkv = share_rows(over_rows(normed, d_proj))
    grad_q = jnp.swapaxes(grad_qkv[:, :, :qw], 0, 1).reshape(rows_d, QW)
    grad_k = jnp.swapaxes(grad_qkv[::copies, :, qw : qw + HD], 0, 1).reshape(rows_d, KW)
    grad_v = jnp.swapaxes(grad_qkv[::copies, :, qw + HD :], 0, 1).reshape(rows_d, KW)
    grad_qkv = jnp.concatenate([grad_q, grad_k, grad_v], axis=1).astype(f32)
    d_proj_own = lax.all_to_all(d_proj.reshape(S, T, hw), "sp", split_axis=0, concat_axis=0)
    wqkv_all = gather_chunks(wqkv_s, s, S)
    grad_normed = jnp.einsum("stc,sdc->td", d_proj_own, wqkv_all, preferred_element_type=f32)
    _, attn_pull = jax.vjp(rms_scale, x_own.astype(f32), g_attn)
    grad_x, grad_g_attn = attn_pull(grad_normed)
    grad_input = grad_middle + grad_x
    tiny = jnp.concatenate([grad_g_attn, grad_g_ffn, grad_g_query, grad_g_key])
    tiny = lax.psum(tiny, ("sp", "fsdp"))
    mine = (s * F + lax.axis_index("fsdp")) * rows_d
    return (
        out[None],
        grad_input[None],
        grad_qkv,
        grad_out,
        grad_gate,
        grad_up,
        grad_down,
        lax.dynamic_slice_in_dim(tiny[:D], mine, rows_d, 0),
        lax.dynamic_slice_in_dim(tiny[D : 2 * D], mine, rows_d, 0),
        tiny[2 * D : 2 * D + HD],
        tiny[2 * D + HD :],
    )


def solution(mesh):
    row = P("fsdp", "sp", None)
    shard = P("fsdp", None)
    grad = P(("sp", "fsdp"), None)
    return jax.shard_map(
        local,
        mesh=mesh,
        in_specs=(
            row,
            shard,
            row,
            shard,
            shard,
            shard,
            shard,
            shard,
            P("fsdp"),
            P("fsdp"),
            P(),
            P(),
        ),
        out_specs=(
            row,
            row,
            grad,
            grad,
            grad,
            grad,
            grad,
            P(("sp", "fsdp")),
            P(("sp", "fsdp")),
            P(),
            P(),
        ),
        check_vma=False,
    )
```

profile of v0, /device:TPU:0, one launch (start us, length us, event | category | flops | bytes accessed | tf_op | source)
XLA Modules:
  0.0 656.7 jit_solution(212468918248744938)
XLA Ops:
  16.5 11.6 %collective-permute-start = (bf16[256,2048]{1,0:T(8,128)(2,1)S(1)}, bf16[256,2048]{1,0:T(8,128)(2,1)}, u32[]{:S(2)}, u32[]{:S(2)}) collective-permute-start(bf16[256,2048]{1,0:T(8,128)(2,1)S(1)} %bitcast.265), channel_id=1, source_target_pairs={{0,8},{8,0},{16,24},{24,16},{1,9},{9,1},{17,25},{25,17},{2,10},{10... | collective-permute-start | bytes 3145736 | tf_op jit(solution)/shard_map/ppermute | solution.py:72
  44.9 21.8 %collective-permute-done.1 = bf16[256,2048]{1,0:T(8,128)(2,1)} collective-permute-done((bf16[256,2048]{1,0:T(8,128)(2,1)S(1)}, bf16[256,2048]{1,0:T(8,128)(2,1)}, u32[]{:S(2)}, u32[]{:S(2)}) %collective-permute-start.1) | collective-permute-done | bytes 1048608 | tf_op jit(solution)/shard_map/ppermute | solution.py:72
  67.8 16.5 %collective-permute-start.3 = (bf16[128,2048]{1,0:T(8,128)(2,1)S(1)}, bf16[128,2048]{1,0:T(8,128)(2,1)S(1)}, u32[]{:S(2)}, u32[]{:S(2)}) collective-permute-start(bf16[128,2048]{1,0:T(8,128)(2,1)S(1)} %slice.186), channel_id=1, source_target_pairs={{0,8},{8,0},{16,24},{24,16},{1,9},{9,1},{17,25},{25,17},{2,10},{10... | collective-permute-start | bytes 1572872 | tf_op jit(solution)/shard_map/ppermute | solution.py:72
  117.3 16.3 %collective-permute-done.10 = bf16[256,2048]{1,0:T(8,128)(2,1)S(1)} collective-permute-done((bf16[256,2048]{1,0:T(8,128)(2,1)}, bf16[256,2048]{1,0:T(8,128)(2,1)S(1)}, u32[]{:S(2)}, u32[]{:S(2)}) %collective-permute-start.10) | collective-permute-done | bytes 1048608 | tf_op jit(solution)/shard_map/ppermute | solution.py:72
  145.8 7.9 %fusion.108 = (f32[4,1024]{1,0:T(4,128)S(1)}, f32[4,1024,1024]{1,2,0:T(8,128)}) fusion(bf16[1024,4,32]{0,2,1:T(8,128)(2,1)S(1)} %get-tuple-element.39, bf16[1024,4,32]{0,2,1:T(8,128)(2,1)S(1)} %get-tuple-element.38, bf16[1024,32]{0,1:T(8,128)(2,1)S(1)} %get-tuple-element.51, bf16[1024,32]{0,1:T(8,128)(2,1)S(1)} %get-tuple-element.50, ...), kind=kOutput, calls=%fused_computation.228 | convolution fusion | flops 550760448 | bytes 18497536 | tf_op jit(solution)/shard_map/qgd,td->gqt/dot_general | solution.py:41
  153.7 8.1 %fusion.4 = f32[4,1024]{1,0:T(4,128)S(1)} fusion(f32[4,1024,1024]{1,2,0:T(8,128)} %get-tuple-element.61, f32[4,1024]{1,0:T(4,128)S(1)} %get-tuple-element.60), kind=kLoop, calls=%fused_computation.10 | loop fusion | flops 8384512 | bytes 16809984 | tf_op jit(solution)/shard_map/reduce_sum | solution.py:52
  178.1 8.0 %collective-permute-done.5 = bf16[1024,256]{1,0:T(8,128)(2,1)} collective-permute-done((bf16[1024,256]{1,0:T(8,128)(2,1)}, bf16[1024,256]{1,0:T(8,128)(2,1)}, u32[]{:S(2)}, u32[]{:S(2)}) %collective-permute-start.5) | collective-permute-done | bytes 524320 | tf_op jit(solution)/shard_map/ppermute | solution.py:72
  195.2 9.9 %multiply_reduce_fusion = (f32[1024]{0:T(1024)S(1)}, f32[1024,2048]{1,0:T(8,128)}) fusion(bf16[4,256,2048]{2,1,0:T(8,128)(2,1)} %fusion.54, bf16[4,1024,256]{2,1,0:T(8,128)(2,1)S(1)} %fusion.62, bf16[4,256,2048]{2,1,0:T(8,128)(2,1)} %fusion.53), kind=kOutput, calls=%fused_computation.22 | convolution fusion | flops 4303354880 | bytes 18878464 | tf_op jit(solution)/shard_map/dot_general | solution.py:191
  205.1 16.0 %fusion.102 = f32[1024,2048]{1,0:T(8,128)} fusion(bf16[2048,2048]{1,0:T(8,128)(2,1)} %all-gather.9.cloned.1.call-done, f32[1024,2048]{1,0:T(8,128)} %get-tuple-element.63, f32[2048]{0:T(1024)S(1)} %get-tuple-element.15, f32[1024]{0:T(1024)S(1)} %add_rsqrt_fusion), kind=kOutput, calls=%fused_computation.223 | convolution fusion | flops 8596226048 | bytes 25178112 | tf_op jit(solution)/shard_map/dot_general | solution.py:193
  221.2 14.7 %fusion.18 = (bf16[1024,1024]{1,0:T(8,128)(2,1)}, bf16[1024,1024]{1,0:T(8,128)(2,1)}, bf16[1024,1024]{1,0:T(8,128)(2,1)}) fusion(f32[1024,2048]{1,0:T(8,128)} %fusion.102, bf16[1024,2048]{1,0:T(8,128)(2,1)} %bitcast.31, bf16[1024,2048]{1,0:T(8,128)(2,1)} %all-gather.11.cloned.1.call-done), kind=kOutput, calls=%fused_computation.30 | convolution fusion | flops 4311744512 | bytes 23068672 | tf_op jit(solution)/shard_map/dot_general | solution.py:36
  235.9 10.9 %fusion.21 = f32[1024,2048]{1,0:T(8,128)S(1)} fusion(bf16[2048,2048]{1,0:T(8,128)(2,1)S(1)} %copy-done.50, bf16[1024,1024]{1,0:T(8,128)(2,1)} %get-tuple-element.25, bf16[1024,1024]{1,0:T(8,128)(2,1)} %get-tuple-element.24), kind=kOutput, calls=%fused_computation.48 | convolution fusion | flops 8598323200 | bytes 20971520 | tf_op jit(solution)/shard_map/dot_general | solution.py:36
  265.6 7.7 %collective-permute-done.14 = bf16[128,2048]{1,0:T(8,128)(2,1)S(1)} collective-permute-done((bf16[128,2048]{1,0:T(8,128)(2,1)S(1)}, bf16[128,2048]{1,0:T(8,128)(2,1)S(1)}, u32[]{:S(2)}, u32[]{:S(2)}) %collective-permute-start.14) | collective-permute-done | bytes 524320 | tf_op jit(solution)/shard_map/ppermute | solution.py:72
  280.9 14.9 %collective-permute-done.25 = bf16[256,2048]{1,0:T(8,128)(2,1)S(1)} collective-permute-done((bf16[256,2048]{1,0:T(8,128)(2,1)}, bf16[256,2048]{1,0:T(8,128)(2,1)S(1)}, u32[]{:S(2)}, u32[]{:S(2)}) %collective-permute-start.25) | collective-permute-done | bytes 1048608 | tf_op jit(solution)/shard_map/ppermute | solution.py:72
  297.6 17.4 %collective-permute-done.17 = bf16[256,2048]{1,0:T(8,128)(2,1)} collective-permute-done((bf16[256,2048]{1,0:T(8,128)(2,1)}, bf16[256,2048]{1,0:T(8,128)(2,1)}, u32[]{:S(2)}, u32[]{:S(2)}) %collective-permute-start.17) | collective-permute-done | bytes 1048608 | tf_op jit(solution)/shard_map/ppermute | solution.py:72
  348.1 8.1 %fusion.85 = f32[1024,1024,4]{1,0,2:T(8,128)} fusion(bf16[1024,4,64]{0,2,1:T(8,128)(2,1)S(1)} %reshape.378, f32[1024,384]{0,1:T(8,128)S(1)} %fusion.100), kind=kOutput, calls=%fused_computation.185 | convolution fusion | flops 536870912 | bytes 17432576 | tf_op jit(solution)/shard_map/qgd,td->gqt/dot_general | solution.py:62
  356.3 8.4 %fusion.42 = bf16[1024,64]{0,1:T(8,128)(2,1)S(1)} fusion(bf16[1024,4,64]{0,2,1:T(8,128)(2,1)S(1)} %reshape.378, f32[4,1024,1024]{1,2,0:T(8,128)} %get-tuple-element.61, f32[4,1024]{1,0:T(4,128)S(1)} %log_add_fusion), kind=kOutput, calls=%fused_computation.81 | convolution fusion | flops 545325056 | bytes 17448960 | tf_op jit(solution)/shard_map/gqt,qgd->td/dot_general | solution.py:61
  364.7 23.8 %fusion.46 = f32[1024,1,64]{0,2,1:T(8,128)S(1)} fusion(f32[1024,1024,4]{1,0,2:T(8,128)} %fusion.85, f32[4,1024,1024]{1,2,0:T(8,128)} %get-tuple-element.61, f32[4,1024]{1,0:T(4,128)S(1)} %log_add_fusion, pred[1024,1024]{0,1:T(8,128)(4,1)} %fusion.20, bf16[1024,4,32]{0,2,1:T(8,128)(2,1)} %copy-done.25, bf16[1024,4,32]{0,2,1:T(8,128)(2,1)S(1)} %get-tuple-element.38), kind=kOutput, calls=%fused_computation.83 | convolution fusion | flops 567481344 | bytes 35405824 | tf_op jit(solution)/shard_map/gqt,qgd->td/dot_general | solution.py:67
  388.6 27.0 %fusion.34 = f32[1024,4,64]{0,2,1:T(8,128)} fusion(f32[1024,1024,4]{1,0,2:T(8,128)} %fusion.85, f32[4,1024,1024]{1,2,0:T(8,128)} %get-tuple-element.61, f32[4,1024]{1,0:T(4,128)} %copy-done.26, pred[1024,1024]{0,1:T(8,128)(4,1)} %fusion.20, bf16[1024,32]{0,1:T(8,128)(2,1)S(1)} %copy-done.39, bf16[1024,32]{0,1:T(8,128)(2,1)S(1)} %copy-done.37), kind=kOutput, calls=%fused_computation.74 | convolution fusion | flops 567284736 | bytes 35799040 | tf_op jit(solution)/shard_map/gqt,td->qgd/dot_general | solution.py:66
  426.9 15.1 %convolution_convert_fusion = bf16[2048,2048]{1,0:T(8,128)(2,1)} fusion(bf16[1024,1024]{1,0:T(8,128)(2,1)} %get-tuple-element.25, bf16[1024,1024]{1,0:T(8,128)(2,1)} %get-tuple-element.24, f32[1024,2048]{1,0:T(8,128)} %get-tuple-element.63, f32[2048]{0:T(1024)S(1)} %copy-done.33, f32[1024]{0:T(1024)S(1)} %copy-done.48), kind=kOutput, calls=%fused_computation.26 | convolution fusion | flops 8608808960 | bytes 20983808 | tf_op jit(solution)/shard_map/dot_general | solution.py:32
  442.0 8.4 %copy.92 = bf16[4,8,64,2048]{3,2,0,1:T(8,128)(2,1)} copy(bf16[4,8,64,2048]{3,2,1,0:T(8,128)(2,1)} %bitcast.267) | data formatting | bytes 16777216 | tf_op jit(solution)/shard_map/reshape | solution.py:209
  452.6 20.1 %collective-permute-done.31 = bf16[256,2048]{1,0:T(8,128)(2,1)S(1)} collective-permute-done((bf16[256,2048]{1,0:T(8,128)(2,1)}, bf16[256,2048]{1,0:T(8,128)(2,1)S(1)}, u32[]{:S(2)}, u32[]{:S(2)}) %collective-permute-start.31) | collective-permute-done | bytes 1048608 | tf_op jit(solution)/shard_map/ppermute | solution.py:72
  491.3 8.6 %convolution_convert_fusion.1 = bf16[1024,2048]{1,0:T(8,128)(2,1)} fusion(bf16[1024,1024]{1,0:T(8,128)(2,1)S(1)} %copy-done.54, bf16[1024,2048]{1,0:T(8,128)(2,1)} %bitcast.31), kind=kOutput, calls=%fused_computation.39 | convolution fusion | flops 4297064448 | bytes 10485760 | tf_op jit(solution)/shard_map/dot_general | solution.py:32
  511.3 22.3 %collective-permute-done.27 = bf16[2048,384]{1,0:T(8,128)(2,1)} collective-permute-done((bf16[2048,384]{1,0:T(8,128)(2,1)}, bf16[2048,384]{1,0:T(8,128)(2,1)}, u32[]{:S(2)}, u32[]{:S(2)}) %collective-permute-start.27) | collective-permute-done | bytes 1572896 | tf_op jit(solution)/shard_map/ppermute | solution.py:72
  565.3 52.6 %psum.7 = f32[4224]{0:T(1024)S(1)} all-reduce(f32[4224]{0:T(1024)S(1)} %concatenate.101), channel_id=1, replica_groups=mesh['sp'=4,'fsdp'=8] {'sp','fsdp'}, use_global_device_ids=true, to_apply=%region_21.22 | all-reduce | flops 4224 | bytes 33792 | tf_op jit(solution)/shard_map/psum | solution.py:254
  (340 shorter events, 265.1 us)
Async XLA Ops:
  7.2 96.6 %all-gather.7.cloned.1.call-start = ((), (), s32[]{:S(2)}) async-start(), calls=%async_computation.9 | async-start | bytes 1179648 | tf_op jit(solution)/shard_map/all_gather | solution.py:149
  9.8 126.9 %all-gather.5.cloned.1.call-start = ((), (), s32[]{:S(2)}) async-start(), calls=%async_computation.8 | async-start | bytes 2359296 | tf_op jit(solution)/shard_map/all_gather | solution.py:149
  14.1 191.0 %all-gather.9.cloned.1.call-start = ((), (), s32[]{:S(2)}) async-start(), calls=%async_computation.10 | async-start | bytes 9437184 | tf_op jit(solution)/shard_map/all_gather | solution.py:149
  16.5 204.7 %all-gather.11.cloned.1.call-start = ((), (), s32[]{:S(2)}) async-start(), calls=%async_computation.11 | async-start | bytes 4718592 | tf_op jit(solution)/shard_map/all_gather | solution.py:149
  16.5 67.8 %collective-permute-start = (bf16[256,2048]{1,0:T(8,128)(2,1)S(1)}, bf16[256,2048]{1,0:T(8,128)(2,1)}, u32[]{:S(2)}, u32[]{:S(2)}) collective-permute-start(bf16[256,2048]{1,0:T(8,128)(2,1)S(1)} %bitcast.265), channel_id=1, source_target_pairs={{0,8},{8,0},{16,24},{24,16},{1,9},{9,1},{17,25},{25,17},{2,10},{10... | collective-permute-start | bytes 3145736 | tf_op jit(solution)/shard_map/ppermute | solution.py:72
  28.2 38.6 %collective-permute-start.1 = (bf16[256,2048]{1,0:T(8,128)(2,1)S(1)}, bf16[256,2048]{1,0:T(8,128)(2,1)}, u32[]{:S(2)}, u32[]{:S(2)}) collective-permute-start(bf16[256,2048]{1,0:T(8,128)(2,1)S(1)} %bitcast.266), channel_id=1, source_target_pairs={{0,16},{8,24},{16,0},{24,8},{1,17},{9,25},{17,1},{25,9},{2,18},{10... | collective-permute-start | bytes 3145736 | tf_op jit(solution)/shard_map/ppermute | solution.py:72
  31.9 57.0 %collective-permute-start.18 = (bf16[256,2048]{1,0:T(8,128)(2,1)}, bf16[256,2048]{1,0:T(8,128)(2,1)}, u32[]{:S(2)}, u32[]{:S(2)}) collective-permute-start(bf16[256,2048]{1,0:T(8,128)(2,1)} %bitcast.269), channel_id=1, source_target_pairs={{0,8},{8,0},{16,24},{24,16},{1,9},{9,1},{17,25},{25,17},{2,10},{10... | collective-permute-start | bytes 3145736 | tf_op jit(solution)/shard_map/ppermute | solution.py:72
  32.0 54.7 %collective-permute-start.19 = (bf16[256,2048]{1,0:T(8,128)(2,1)}, bf16[256,2048]{1,0:T(8,128)(2,1)}, u32[]{:S(2)}, u32[]{:S(2)}) collective-permute-start(bf16[256,2048]{1,0:T(8,128)(2,1)} %bitcast.270), channel_id=1, source_target_pairs={{0,16},{8,24},{16,0},{24,8},{1,17},{9,25},{17,1},{25,9},{2,18},{10... | collective-permute-start | bytes 3145736 | tf_op jit(solution)/shard_map/ppermute | solution.py:72
  67.8 34.9 %collective-permute-start.3 = (bf16[128,2048]{1,0:T(8,128)(2,1)S(1)}, bf16[128,2048]{1,0:T(8,128)(2,1)S(1)}, u32[]{:S(2)}, u32[]{:S(2)}) collective-permute-start(bf16[128,2048]{1,0:T(8,128)(2,1)S(1)} %slice.186), channel_id=1, source_target_pairs={{0,8},{8,0},{16,24},{24,16},{1,9},{9,1},{17,25},{25,17},{2,10},{10... | collective-permute-start | bytes 1572872 | tf_op jit(solution)/shard_map/ppermute | solution.py:72
  103.9 30.5 %collective-permute-start.9 = (bf16[256,2048]{1,0:T(8,128)(2,1)}, bf16[256,2048]{1,0:T(8,128)(2,1)S(1)}, u32[]{:S(2)}, u32[]{:S(2)}) collective-permute-start(bf16[256,2048]{1,0:T(8,128)(2,1)} %all-gather.7.cloned.1.call-done), channel_id=1, source_target_pairs={{0,8},{8,0},{16,24},{24,16},{1,9},{9,1},{17,25},{25,17},{2,10},{10... | collective-permute-start | bytes 3145736 | tf_op jit(solution)/shard_map/ppermute | solution.py:72
  105.5 28.0 %collective-permute-start.10 = (bf16[256,2048]{1,0:T(8,128)(2,1)}, bf16[256,2048]{1,0:T(8,128)(2,1)S(1)}, u32[]{:S(2)}, u32[]{:S(2)}) collective-permute-start(bf16[256,2048]{1,0:T(8,128)(2,1)} %all-gather.7.cloned.1.call-done), channel_id=1, source_target_pairs={{0,16},{8,24},{16,0},{24,8},{1,17},{9,25},{17,1},{25,9},{2,18},{10... | collective-permute-start | bytes 3145736 | tf_op jit(solution)/shard_map/ppermute | solution.py:72
  134.4 40.9 %collective-permute-start.12 = (bf16[128,2048]{1,0:T(8,128)(2,1)}, bf16[128,2048]{1,0:T(8,128)(2,1)}, u32[]{:S(2)}, u32[]{:S(2)}) collective-permute-start(bf16[128,2048]{1,0:T(8,128)(2,1)} %slice.199), channel_id=1, source_target_pairs={{0,8},{8,0},{16,24},{24,16},{1,9},{9,1},{17,25},{25,17},{2,10},{10... | collective-permute-start | bytes 1572872 | tf_op jit(solution)/shard_map/ppermute | solution.py:72
  135.2 40.1 %collective-permute-start.11 = (bf16[128,2048]{1,0:T(8,128)(2,1)}, bf16[128,2048]{1,0:T(8,128)(2,1)}, u32[]{:S(2)}, u32[]{:S(2)}) collective-permute-start(bf16[128,2048]{1,0:T(8,128)(2,1)} %slice.198), channel_id=1, source_target_pairs={{0,16},{8,24},{16,0},{24,8},{1,17},{9,25},{17,1},{25,9},{2,18},{10... | collective-permute-start | bytes 1572872 | tf_op jit(solution)/shard_map/ppermute | solution.py:72
  262.9 32.9 %collective-permute-start.25 = (bf16[256,2048]{1,0:T(8,128)(2,1)}, bf16[256,2048]{1,0:T(8,128)(2,1)S(1)}, u32[]{:S(2)}, u32[]{:S(2)}) collective-permute-start(bf16[256,2048]{1,0:T(8,128)(2,1)} %pad_maximum_fusion.7), channel_id=1, source_target_pairs={{0,16},{8,24},{16,0},{24,8},{1,17},{9,25},{17,1},{25,9},{2,18},{10... | collective-permute-start | bytes 3145736 | tf_op jit(solution)/shard_map/ppermute | solution.py:72
  264.6 33.0 %collective-permute-start.23 = (bf16[256,2048]{1,0:T(8,128)(2,1)}, bf16[256,2048]{1,0:T(8,128)(2,1)}, u32[]{:S(2)}, u32[]{:S(2)}) collective-permute-start(bf16[256,2048]{1,0:T(8,128)(2,1)} %pad_maximum_fusion.6), channel_id=1, source_target_pairs={{0,8},{8,0},{16,24},{24,16},{1,9},{9,1},{17,25},{25,17},{2,10},{10... | collective-permute-start | bytes 3145736 | tf_op jit(solution)/shard_map/ppermute | solution.py:72
  276.3 38.6 %collective-permute-start.17 = (bf16[256,2048]{1,0:T(8,128)(2,1)}, bf16[256,2048]{1,0:T(8,128)(2,1)}, u32[]{:S(2)}, u32[]{:S(2)}) collective-permute-start(bf16[256,2048]{1,0:T(8,128)(2,1)} %pad_maximum_fusion.5), channel_id=1, source_target_pairs={{0,16},{8,24},{16,0},{24,8},{1,17},{9,25},{17,1},{25,9},{2,18},{10... | collective-permute-start | bytes 3145736 | tf_op jit(solution)/shard_map/ppermute | solution.py:72
  277.7 38.7 %collective-permute-start.15 = (bf16[256,2048]{1,0:T(8,128)(2,1)}, bf16[256,2048]{1,0:T(8,128)(2,1)}, u32[]{:S(2)}, u32[]{:S(2)}) collective-permute-start(bf16[256,2048]{1,0:T(8,128)(2,1)} %pad_maximum_fusion.4), channel_id=1, source_target_pairs={{0,8},{8,0},{16,24},{24,16},{1,9},{9,1},{17,25},{25,17},{2,10},{10... | collective-permute-start | bytes 3145736 | tf_op jit(solution)/shard_map/ppermute | solution.py:72
  339.1 282.9 %reduce-scatter.5.cloned.1.call-start = ((), (), s32[]{:S(2)}) async-start(), calls=%async_computation.12 | async-start | bytes 1769472 | tf_op jit(solution)/shard_map/reduce_scatter | solution.py:211
  426.8 204.8 %reduce-scatter.9.cloned.1.call-start = ((), (), s32[]{:S(2)}) async-start(), calls=%async_computation.14 | async-start | bytes 9437184 | tf_op jit(solution)/shard_map/reduce_scatter | solution.py:211
  450.5 186.5 %reduce-scatter.7.cloned.1.call-start = ((), (), s32[]{:S(2)}) async-start(), calls=%async_computation.13 | async-start | bytes 1179648 | tf_op jit(solution)/shard_map/reduce_scatter | solution.py:231
  452.1 24.2 %collective-permute-start.30 = (bf16[256,2048]{1,0:T(8,128)(2,1)}, bf16[256,2048]{1,0:T(8,128)(2,1)S(1)}, u32[]{:S(2)}, u32[]{:S(2)}) collective-permute-start(bf16[256,2048]{1,0:T(8,128)(2,1)} %get-tuple-element.22), channel_id=1, source_target_pairs={{0,8},{8,0},{16,24},{24,16},{1,9},{9,1},{17,25},{25,17},{2,10},{10... | collective-permute-start | bytes 3145736 | tf_op jit(solution)/shard_map/ppermute | solution.py:72
  491.3 150.1 %reduce-scatter.11.cloned.1.call-start = ((), (), s32[]{:S(2)}) async-start(), calls=%async_computation.15 | async-start | bytes 4718592 | tf_op jit(solution)/shard_map/reduce_scatter | solution.py:202
  502.7 30.8 %collective-permute-start.27 = (bf16[2048,384]{1,0:T(8,128)(2,1)}, bf16[2048,384]{1,0:T(8,128)(2,1)}, u32[]{:S(2)}, u32[]{:S(2)}) collective-permute-start(bf16[2048,384]{1,0:T(8,128)(2,1)} %slice.188), channel_id=1, source_target_pairs={{0,16},{8,24},{16,0},{24,8},{1,17},{9,25},{17,1},{25,9},{2,18},{10... | collective-permute-start | bytes 4718600 | tf_op jit(solution)/shard_map/ppermute | solution.py:72
  502.8 33.0 %collective-permute-start.26 = (bf16[2048,384]{1,0:T(8,128)(2,1)}, bf16[2048,384]{1,0:T(8,128)(2,1)}, u32[]{:S(2)}, u32[]{:S(2)}) collective-permute-start(bf16[2048,384]{1,0:T(8,128)(2,1)} %slice.188), channel_id=1, source_target_pairs={{0,8},{8,0},{16,24},{24,16},{1,9},{9,1},{17,25},{25,17},{2,10},{10... | collective-permute-start | bytes 4718600 | tf_op jit(solution)/shard_map/ppermute | solution.py:72
  (77 other events, 1695.0 us)
Sparse Core Ops, SparseCore 0:
  10.2 43.0 all-gather.6
  55.5 30.0 all-gather.4
  87.8 81.5 all-gather.8
  170.8 45.6 all-gather.10
  427.0 39.8 reduce-scatter.4
  469.0 87.4 reduce-scatter.8
  559.4 30.5 reduce-scatter.6
  592.2 49.0 reduce-scatter.10
where the time goes:
time: 667 us; the launch traced here: 657 us
  matrix products  184 us (28%)
  waiting for transfers between devices  170 us (25%)
  local copies, waits for them, and re-layouts  87.9 us (13%)
  starting transfers between devices  79.1 us (12%)
  other arithmetic  67.2 us (10%)
  blocking collectives  52.6 us (8%)
  between operations  15.6 us (2%)
    ppermute x32, waiting for transfers between devices, swap(): return lax.ppermute(value, 'sp', [(i, i ^ mask) for i in range(count)])  153 us
    ppermute x32, starting transfers between devices, swap(): return lax.ppermute(value, 'sp', [(i, i ^ mask) for i in range(count)])  60.9 us
    psum x1, blocking collectives, local(): tiny = lax.psum(tiny, ('sp', 'fsdp'))  52.6 us
    dot_general x3, matrix products, times_transposed(): lax.dot_general(a, b, (((1,), (1,)), ((), ())), preferred_element_type=f32)  30.9 us
    dot_general x4, matrix products, over_rows(): lax.dot_general(a, b, (((0,), (0,)), ((), ())), preferred_element_type=f32)  30.7 us
    dynamic_update_slice x17, local copies, waits for them, and re-layouts, gather_chunks(): stack = lax.dynamic_update_slice_in_dim(stack, part[None], s ^ mask, 0)  27.5 us
    dot_general x1, matrix products, attend_back(): jnp.einsum('gqt,td->qgd', grad_s, k, preferred_element_type=f32) * scale  27 us
    dot_general x1, matrix products, attend_back(): jnp.einsum('gqt,qgd->td', grad_s, q, preferred_element_type=f32) * scale  23.8 us
  transfers between devices with their start and end apart: 46, of which 25 were waited for; matrix products, arithmetic and copies ran while one was open for 31% of the time, Pallas kernels for 0%

commit v1 on v0

--- a/solution.py
+++ b/solution.py
@@ -251,7 +251,7 @@
     grad_x, grad_g_attn = attn_pull(grad_normed)
     grad_input = grad_middle + grad_x
     tiny = jnp.concatenate([grad_g_attn, grad_g_ffn, grad_g_query, grad_g_key])
-    tiny = lax.psum(tiny, ("sp", "fsdp"))
+    tiny = jax.lax.psum(jax.lax.psum(tiny, "fsdp"), "sp")
     mine = (s * F + lax.axis_index("fsdp")) * rows_d
     return (
         out[None],

time: 667 us -> 663 us (level)
    psum x1 -> x2, blocking collectives: 52.6 us -> 52.2 us  [local(): tiny = jax.lax.psum(jax.lax.psum(tiny, 'fsdp'), 'sp')]
where the time goes in v1:
time: 663 us; the launch traced here: 653 us
  matrix products  184 us (28%)
  waiting for transfers between devices  168 us (25%)
  local copies, waits for them, and re-layouts  87.8 us (13%)
  starting transfers between devices  77.8 us (12%)
  other arithmetic  67.1 us (10%)
  blocking collectives  52.2 us (8%)
  between operations  15.6 us (2%)
    ppermute x32, waiting for transfers between devices, swap(): return lax.ppermute(value, 'sp', [(i, i ^ mask) for i in range(count)])  154 us
    ppermute x32, starting transfers between devices, swap(): return lax.ppermute(value, 'sp', [(i, i ^ mask) for i in range(count)])  60.7 us
    psum x2, blocking collectives, local(): tiny = jax.lax.psum(jax.lax.psum(tiny, 'fsdp'), 'sp')  52.2 us
    dot_general x3, matrix products, times_transposed(): lax.dot_general(a, b, (((1,), (1,)), ((), ())), preferred_element_type=f32)  30.9 us
    dot_general x4, matrix products, over_rows(): lax.dot_general(a, b, (((0,), (0,)), ((), ())), preferred_element_type=f32)  30.8 us
    dynamic_update_slice x17, local copies, waits for them, and re-layouts, gather_chunks(): stack = lax.dynamic_update_slice_in_dim(stack, part[None], s ^ mask, 0)  27.4 us
    dot_general x1, matrix products, attend_back(): jnp.einsum('gqt,td->qgd', grad_s, k, preferred_element_type=f32) * scale  27.3 us
    dot_general x1, matrix products, attend_back(): jnp.einsum('gqt,qgd->td', grad_s, q, preferred_element_type=f32) * scale  23.8 us
  transfers between devices with their start and end apart: 46, of which 25 were waited for; matrix products, arithmetic and copies ran while one was open for 31% of the time, Pallas kernels for 0%

profile of v1, /device:TPU:0, one launch (start us, length us, event | category | flops | bytes accessed | tf_op | source)
XLA Modules:
  0.0 652.9 jit_solution(2754737519687339180)
XLA Ops:
  16.5 11.6 %collective-permute-start = (bf16[256,2048]{1,0:T(8,128)(2,1)S(1)}, bf16[256,2048]{1,0:T(8,128)(2,1)}, u32[]{:S(2)}, u32[]{:S(2)}) collective-permute-start(bf16[256,2048]{1,0:T(8,128)(2,1)S(1)} %bitcast.265), channel_id=1, source_target_pairs={{0,8},{8,0},{16,24},{24,16},{1,9},{9,1},{17,25},{25,17},{2,10},{10... | collective-permute-start | bytes 3145736 | tf_op jit(solution)/shard_map/ppermute | solution.py:72
  44.9 21.8 %collective-permute-done.1 = bf16[256,2048]{1,0:T(8,128)(2,1)} collective-permute-done((bf16[256,2048]{1,0:T(8,128)(2,1)S(1)}, bf16[256,2048]{1,0:T(8,128)(2,1)}, u32[]{:S(2)}, u32[]{:S(2)}) %collective-permute-start.1) | collective-permute-done | bytes 1048608 | tf_op jit(solution)/shard_map/ppermute | solution.py:72
  67.8 16.5 %collective-permute-start.3 = (bf16[128,2048]{1,0:T(8,128)(2,1)S(1)}, bf16[128,2048]{1,0:T(8,128)(2,1)S(1)}, u32[]{:S(2)}, u32[]{:S(2)}) collective-permute-start(bf16[128,2048]{1,0:T(8,128)(2,1)S(1)} %slice.186), channel_id=1, source_target_pairs={{0,8},{8,0},{16,24},{24,16},{1,9},{9,1},{17,25},{25,17},{2,10},{10... | collective-permute-start | bytes 1572872 | tf_op jit(solution)/shard_map/ppermute | solution.py:72
  117.3 16.3 %collective-permute-done.10 = bf16[256,2048]{1,0:T(8,128)(2,1)S(1)} collective-permute-done((bf16[256,2048]{1,0:T(8,128)(2,1)}, bf16[256,2048]{1,0:T(8,128)(2,1)S(1)}, u32[]{:S(2)}, u32[]{:S(2)}) %collective-permute-start.10) | collective-permute-done | bytes 1048608 | tf_op jit(solution)/shard_map/ppermute | solution.py:72
  145.9 7.9 %fusion.108 = (f32[4,1024]{1,0:T(4,128)S(1)}, f32[4,1024,1024]{1,2,0:T(8,128)}) fusion(bf16[1024,4,32]{0,2,1:T(8,128)(2,1)S(1)} %get-tuple-element.39, bf16[1024,4,32]{0,2,1:T(8,128)(2,1)S(1)} %get-tuple-element.38, bf16[1024,32]{0,1:T(8,128)(2,1)S(1)} %get-tuple-element.51, bf16[1024,32]{0,1:T(8,128)(2,1)S(1)} %get-tuple-element.50, ...), kind=kOutput, calls=%fused_computation.228 | convolution fusion | flops 550760448 | bytes 18497536 | tf_op jit(solution)/shard_map/qgd,td->gqt/dot_general | solution.py:41
  153.8 8.1 %fusion.4 = f32[4,1024]{1,0:T(4,128)S(1)} fusion(f32[4,1024,1024]{1,2,0:T(8,128)} %get-tuple-element.61, f32[4,1024]{1,0:T(4,128)S(1)} %get-tuple-element.60), kind=kLoop, calls=%fused_computation.10 | loop fusion | flops 8384512 | bytes 16809984 | tf_op jit(solution)/shard_map/reduce_sum | solution.py:52
  178.0 8.0 %collective-permute-done.5 = bf16[1024,256]{1,0:T(8,128)(2,1)} collective-permute-done((bf16[1024,256]{1,0:T(8,128)(2,1)}, bf16[1024,256]{1,0:T(8,128)(2,1)}, u32[]{:S(2)}, u32[]{:S(2)}) %collective-permute-start.5) | collective-permute-done | bytes 524320 | tf_op jit(solution)/shard_map/ppermute | solution.py:72
  195.2 9.9 %multiply_reduce_fusion = (f32[1024]{0:T(1024)S(1)}, f32[1024,2048]{1,0:T(8,128)}) fusion(bf16[4,256,2048]{2,1,0:T(8,128)(2,1)} %fusion.54, bf16[4,1024,256]{2,1,0:T(8,128)(2,1)S(1)} %fusion.62, bf16[4,256,2048]{2,1,0:T(8,128)(2,1)} %fusion.53), kind=kOutput, calls=%fused_computation.22 | convolution fusion | flops 4303354880 | bytes 18878464 | tf_op jit(solution)/shard_map/dot_general | solution.py:191
  205.1 15.9 %fusion.102 = f32[1024,2048]{1,0:T(8,128)} fusion(bf16[2048,2048]{1,0:T(8,128)(2,1)} %all-gather.9.cloned.1.call-done, f32[1024,2048]{1,0:T(8,128)} %get-tuple-element.63, f32[2048]{0:T(1024)S(1)} %get-tuple-element.15, f32[1024]{0:T(1024)S(1)} %add_rsqrt_fusion), kind=kOutput, calls=%fused_computation.223 | convolution fusion | flops 8596226048 | bytes 25178112 | tf_op jit(solution)/shard_map/dot_general | solution.py:193
  221.0 14.7 %fusion.18 = (bf16[1024,1024]{1,0:T(8,128)(2,1)}, bf16[1024,1024]{1,0:T(8,128)(2,1)}, bf16[1024,1024]{1,0:T(8,128)(2,1)}) fusion(f32[1024,2048]{1,0:T(8,128)} %fusion.102, bf16[1024,2048]{1,0:T(8,128)(2,1)} %bitcast.31, bf16[1024,2048]{1,0:T(8,128)(2,1)} %all-gather.11.cloned.1.call-done), kind=kOutput, calls=%fused_computation.30 | convolution fusion | flops 4311744512 | bytes 23068672 | tf_op jit(solution)/shard_map/dot_general | solution.py:36
  235.7 10.9 %fusion.21 = f32[1024,2048]{1,0:T(8,128)S(1)} fusion(bf16[2048,2048]{1,0:T(8,128)(2,1)S(1)} %copy-done.50, bf16[1024,1024]{1,0:T(8,128)(2,1)} %get-tuple-element.25, bf16[1024,1024]{1,0:T(8,128)(2,1)} %get-tuple-element.24), kind=kOutput, calls=%fused_computation.48 | convolution fusion | flops 8598323200 | bytes 20971520 | tf_op jit(solution)/shard_map/dot_general | solution.py:36
  280.7 14.9 %collective-permute-done.25 = bf16[256,2048]{1,0:T(8,128)(2,1)S(1)} collective-permute-done((bf16[256,2048]{1,0:T(8,128)(2,1)}, bf16[256,2048]{1,0:T(8,128)(2,1)S(1)}, u32[]{:S(2)}, u32[]{:S(2)}) %collective-permute-start.25) | collective-permute-done | bytes 1048608 | tf_op jit(solution)/shard_map/ppermute | solution.py:72
  297.4 17.4 %collective-permute-done.17 = bf16[256,2048]{1,0:T(8,128)(2,1)} collective-permute-done((bf16[256,2048]{1,0:T(8,128)(2,1)}, bf16[256,2048]{1,0:T(8,128)(2,1)}, u32[]{:S(2)}, u32[]{:S(2)}) %collective-permute-start.17) | collective-permute-done | bytes 1048608 | tf_op jit(solution)/shard_map/ppermute | solution.py:72
  348.0 8.1 %fusion.85 = f32[1024,1024,4]{1,0,2:T(8,128)} fusion(bf16[1024,4,64]{0,2,1:T(8,128)(2,1)S(1)} %reshape.378, f32[1024,384]{0,1:T(8,128)S(1)} %fusion.100), kind=kOutput, calls=%fused_computation.185 | convolution fusion | flops 536870912 | bytes 17432576 | tf_op jit(solution)/shard_map/qgd,td->gqt/dot_general | solution.py:62
  356.1 8.4 %fusion.42 = bf16[1024,64]{0,1:T(8,128)(2,1)S(1)} fusion(bf16[1024,4,64]{0,2,1:T(8,128)(2,1)S(1)} %reshape.378, f32[4,1024,1024]{1,2,0:T(8,128)} %get-tuple-element.61, f32[4,1024]{1,0:T(4,128)S(1)} %log_add_fusion), kind=kOutput, calls=%fused_computation.81 | convolution fusion | flops 545325056 | bytes 17448960 | tf_op jit(solution)/shard_map/gqt,qgd->td/dot_general | solution.py:61
  364.6 23.8 %fusion.46 = f32[1024,1,64]{0,2,1:T(8,128)S(1)} fusion(f32[1024,1024,4]{1,0,2:T(8,128)} %fusion.85, f32[4,1024,1024]{1,2,0:T(8,128)} %get-tuple-element.61, f32[4,1024]{1,0:T(4,128)S(1)} %log_add_fusion, pred[1024,1024]{0,1:T(8,128)(4,1)} %fusion.20, bf16[1024,4,32]{0,2,1:T(8,128)(2,1)} %copy-done.25, bf16[1024,4,32]{0,2,1:T(8,128)(2,1)S(1)} %get-tuple-element.38), kind=kOutput, calls=%fused_computation.83 | convolution fusion | flops 567481344 | bytes 35405824 | tf_op jit(solution)/shard_map/gqt,qgd->td/dot_general | solution.py:67
  388.4 27.3 %fusion.34 = f32[1024,4,64]{0,2,1:T(8,128)} fusion(f32[1024,1024,4]{1,0,2:T(8,128)} %fusion.85, f32[4,1024,1024]{1,2,0:T(8,128)} %get-tuple-element.61, f32[4,1024]{1,0:T(4,128)} %copy-done.26, pred[1024,1024]{0,1:T(8,128)(4,1)} %fusion.20, bf16[1024,32]{0,1:T(8,128)(2,1)S(1)} %copy-done.39, bf16[1024,32]{0,1:T(8,128)(2,1)S(1)} %copy-done.37), kind=kOutput, calls=%fused_computation.74 | convolution fusion | flops 567284736 | bytes 35799040 | tf_op jit(solution)/shard_map/gqt,td->qgd/dot_general | solution.py:66
  427.1 15.1 %convolution_convert_fusion = bf16[2048,2048]{1,0:T(8,128)(2,1)} fusion(bf16[1024,1024]{1,0:T(8,128)(2,1)} %get-tuple-element.25, bf16[1024,1024]{1,0:T(8,128)(2,1)} %get-tuple-element.24, f32[1024,2048]{1,0:T(8,128)} %get-tuple-element.63, f32[2048]{0:T(1024)S(1)} %copy-done.33, f32[1024]{0:T(1024)S(1)} %copy-done.48), kind=kOutput, calls=%fused_computation.26 | convolution fusion | flops 8608808960 | bytes 20983808 | tf_op jit(solution)/shard_map/dot_general | solution.py:32
  442.2 8.4 %copy.92 = bf16[4,8,64,2048]{3,2,0,1:T(8,128)(2,1)} copy(bf16[4,8,64,2048]{3,2,1,0:T(8,128)(2,1)} %bitcast.267) | data formatting | bytes 16777216 | tf_op jit(solution)/shard_map/reshape | solution.py:209
  452.8 20.2 %collective-permute-done.31 = bf16[256,2048]{1,0:T(8,128)(2,1)S(1)} collective-permute-done((bf16[256,2048]{1,0:T(8,128)(2,1)}, bf16[256,2048]{1,0:T(8,128)(2,1)S(1)}, u32[]{:S(2)}, u32[]{:S(2)}) %collective-permute-start.31) | collective-permute-done | bytes 1048608 | tf_op jit(solution)/shard_map/ppermute | solution.py:72
  491.5 8.6 %convolution_convert_fusion.1 = bf16[1024,2048]{1,0:T(8,128)(2,1)} fusion(bf16[1024,1024]{1,0:T(8,128)(2,1)S(1)} %copy-done.54, bf16[1024,2048]{1,0:T(8,128)(2,1)} %bitcast.31), kind=kOutput, calls=%fused_computation.39 | convolution fusion | flops 4297064448 | bytes 10485760 | tf_op jit(solution)/shard_map/dot_general | solution.py:32
  511.4 22.4 %collective-permute-done.27 = bf16[2048,384]{1,0:T(8,128)(2,1)} collective-permute-done((bf16[2048,384]{1,0:T(8,128)(2,1)}, bf16[2048,384]{1,0:T(8,128)(2,1)}, u32[]{:S(2)}, u32[]{:S(2)}) %collective-permute-start.27) | collective-permute-done | bytes 1572896 | tf_op jit(solution)/shard_map/ppermute | solution.py:72
  565.7 36.6 %psum.14 = f32[4224]{0:T(1024)S(1)} all-reduce(f32[4224]{0:T(1024)S(1)} %concatenate.101), channel_id=1, replica_groups=mesh['sp'=4,'fsdp'=8] {'fsdp'}, use_global_device_ids=true, to_apply=%region_21.22 | all-reduce | flops 4224 | bytes 33792 | tf_op jit(solution)/shard_map/psum | solution.py:254
  602.3 15.6 %psum.15 = f32[4224]{0:T(1024)S(1)} all-reduce(f32[4224]{0:T(1024)S(1)} %psum.14), channel_id=1, replica_groups=mesh['sp'=4,'fsdp'=8] {'sp'}, use_global_device_ids=true, to_apply=%region_22.23 | all-reduce | flops 4224 | bytes 33792 | tf_op jit(solution)/shard_map/psum | solution.py:254
  (341 shorter events, 268.9 us)
Async XLA Ops:
  7.2 96.6 %all-gather.7.cloned.1.call-start = ((), (), s32[]{:S(2)}) async-start(), calls=%async_computation.9 | async-start | bytes 1179648 | tf_op jit(solution)/shard_map/all_gather | solution.py:149
  9.8 127.0 %all-gather.5.cloned.1.call-start = ((), (), s32[]{:S(2)}) async-start(), calls=%async_computation.8 | async-start | bytes 2359296 | tf_op jit(solution)/shard_map/all_gather | solution.py:149
  14.1 191.1 %all-gather.9.cloned.1.call-start = ((), (), s32[]{:S(2)}) async-start(), calls=%async_computation.10 | async-start | bytes 9437184 | tf_op jit(solution)/shard_map/all_gather | solution.py:149
  16.5 204.5 %all-gather.11.cloned.1.call-start = ((), (), s32[]{:S(2)}) async-start(), calls=%async_computation.11 | async-start | bytes 4718592 | tf_op jit(solution)/shard_map/all_gather | solution.py:149
  16.5 67.8 %collective-permute-start = (bf16[256,2048]{1,0:T(8,128)(2,1)S(1)}, bf16[256,2048]{1,0:T(8,128)(2,1)}, u32[]{:S(2)}, u32[]{:S(2)}) collective-permute-start(bf16[256,2048]{1,0:T(8,128)(2,1)S(1)} %bitcast.265), channel_id=1, source_target_pairs={{0,8},{8,0},{16,24},{24,16},{1,9},{9,1},{17,25},{25,17},{2,10},{10... | collective-permute-start | bytes 3145736 | tf_op jit(solution)/shard_map/ppermute | solution.py:72
  28.2 38.6 %collective-permute-start.1 = (bf16[256,2048]{1,0:T(8,128)(2,1)S(1)}, bf16[256,2048]{1,0:T(8,128)(2,1)}, u32[]{:S(2)}, u32[]{:S(2)}) collective-permute-start(bf16[256,2048]{1,0:T(8,128)(2,1)S(1)} %bitcast.266), channel_id=1, source_target_pairs={{0,16},{8,24},{16,0},{24,8},{1,17},{9,25},{17,1},{25,9},{2,18},{10... | collective-permute-start | bytes 3145736 | tf_op jit(solution)/shard_map/ppermute | solution.py:72
  31.9 57.0 %collective-permute-start.18 = (bf16[256,2048]{1,0:T(8,128)(2,1)}, bf16[256,2048]{1,0:T(8,128)(2,1)}, u32[]{:S(2)}, u32[]{:S(2)}) collective-permute-start(bf16[256,2048]{1,0:T(8,128)(2,1)} %bitcast.269), channel_id=1, source_target_pairs={{0,8},{8,0},{16,24},{24,16},{1,9},{9,1},{17,25},{25,17},{2,10},{10... | collective-permute-start | bytes 3145736 | tf_op jit(solution)/shard_map/ppermute | solution.py:72
  32.0 54.7 %collective-permute-start.19 = (bf16[256,2048]{1,0:T(8,128)(2,1)}, bf16[256,2048]{1,0:T(8,128)(2,1)}, u32[]{:S(2)}, u32[]{:S(2)}) collective-permute-start(bf16[256,2048]{1,0:T(8,128)(2,1)} %bitcast.270), channel_id=1, source_target_pairs={{0,16},{8,24},{16,0},{24,8},{1,17},{9,25},{17,1},{25,9},{2,18},{10... | collective-permute-start | bytes 3145736 | tf_op jit(solution)/shard_map/ppermute | solution.py:72
  67.8 34.9 %collective-permute-start.3 = (bf16[128,2048]{1,0:T(8,128)(2,1)S(1)}, bf16[128,2048]{1,0:T(8,128)(2,1)S(1)}, u32[]{:S(2)}, u32[]{:S(2)}) collective-permute-start(bf16[128,2048]{1,0:T(8,128)(2,1)S(1)} %slice.186), channel_id=1, source_target_pairs={{0,8},{8,0},{16,24},{24,16},{1,9},{9,1},{17,25},{25,17},{2,10},{10... | collective-permute-start | bytes 1572872 | tf_op jit(solution)/shard_map/ppermute | solution.py:72
  103.8 30.6 %collective-permute-start.9 = (bf16[256,2048]{1,0:T(8,128)(2,1)}, bf16[256,2048]{1,0:T(8,128)(2,1)S(1)}, u32[]{:S(2)}, u32[]{:S(2)}) collective-permute-start(bf16[256,2048]{1,0:T(8,128)(2,1)} %all-gather.7.cloned.1.call-done), channel_id=1, source_target_pairs={{0,8},{8,0},{16,24},{24,16},{1,9},{9,1},{17,25},{25,17},{2,10},{10... | collective-permute-start | bytes 3145736 | tf_op jit(solution)/shard_map/ppermute | solution.py:72
  105.5 28.1 %collective-permute-start.10 = (bf16[256,2048]{1,0:T(8,128)(2,1)}, bf16[256,2048]{1,0:T(8,128)(2,1)S(1)}, u32[]{:S(2)}, u32[]{:S(2)}) collective-permute-start(bf16[256,2048]{1,0:T(8,128)(2,1)} %all-gather.7.cloned.1.call-done), channel_id=1, source_target_pairs={{0,16},{8,24},{16,0},{24,8},{1,17},{9,25},{17,1},{25,9},{2,18},{10... | collective-permute-start | bytes 3145736 | tf_op jit(solution)/shard_map/ppermute | solution.py:72
  134.4 40.8 %collective-permute-start.12 = (bf16[128,2048]{1,0:T(8,128)(2,1)}, bf16[128,2048]{1,0:T(8,128)(2,1)}, u32[]{:S(2)}, u32[]{:S(2)}) collective-permute-start(bf16[128,2048]{1,0:T(8,128)(2,1)} %slice.199), channel_id=1, source_target_pairs={{0,8},{8,0},{16,24},{24,16},{1,9},{9,1},{17,25},{25,17},{2,10},{10... | collective-permute-start | bytes 1572872 | tf_op jit(solution)/shard_map/ppermute | solution.py:72
  135.2 40.0 %collective-permute-start.11 = (bf16[128,2048]{1,0:T(8,128)(2,1)}, bf16[128,2048]{1,0:T(8,128)(2,1)}, u32[]{:S(2)}, u32[]{:S(2)}) collective-permute-start(bf16[128,2048]{1,0:T(8,128)(2,1)} %slice.198), channel_id=1, source_target_pairs={{0,16},{8,24},{16,0},{24,8},{1,17},{9,25},{17,1},{25,9},{2,18},{10... | collective-permute-start | bytes 1572872 | tf_op jit(solution)/shard_map/ppermute | solution.py:72
  262.7 32.9 %collective-permute-start.25 = (bf16[256,2048]{1,0:T(8,128)(2,1)}, bf16[256,2048]{1,0:T(8,128)(2,1)S(1)}, u32[]{:S(2)}, u32[]{:S(2)}) collective-permute-start(bf16[256,2048]{1,0:T(8,128)(2,1)} %pad_maximum_fusion.7), channel_id=1, source_target_pairs={{0,16},{8,24},{16,0},{24,8},{1,17},{9,25},{17,1},{25,9},{2,18},{10... | collective-permute-start | bytes 3145736 | tf_op jit(solution)/shard_map/ppermute | solution.py:72
  264.4 33.0 %collective-permute-start.23 = (bf16[256,2048]{1,0:T(8,128)(2,1)}, bf16[256,2048]{1,0:T(8,128)(2,1)}, u32[]{:S(2)}, u32[]{:S(2)}) collective-permute-start(bf16[256,2048]{1,0:T(8,128)(2,1)} %pad_maximum_fusion.6), channel_id=1, source_target_pairs={{0,8},{8,0},{16,24},{24,16},{1,9},{9,1},{17,25},{25,17},{2,10},{10... | collective-permute-start | bytes 3145736 | tf_op jit(solution)/shard_map/ppermute | solution.py:72
  276.2 38.6 %collective-permute-start.17 = (bf16[256,2048]{1,0:T(8,128)(2,1)}, bf16[256,2048]{1,0:T(8,128)(2,1)}, u32[]{:S(2)}, u32[]{:S(2)}) collective-permute-start(bf16[256,2048]{1,0:T(8,128)(2,1)} %pad_maximum_fusion.5), channel_id=1, source_target_pairs={{0,16},{8,24},{16,0},{24,8},{1,17},{9,25},{17,1},{25,9},{2,18},{10... | collective-permute-start | bytes 3145736 | tf_op jit(solution)/shard_map/ppermute | solution.py:72
  277.6 38.7 %collective-permute-start.15 = (bf16[256,2048]{1,0:T(8,128)(2,1)}, bf16[256,2048]{1,0:T(8,128)(2,1)}, u32[]{:S(2)}, u32[]{:S(2)}) collective-permute-start(bf16[256,2048]{1,0:T(8,128)(2,1)} %pad_maximum_fusion.4), channel_id=1, source_target_pairs={{0,8},{8,0},{16,24},{24,16},{1,9},{9,1},{17,25},{25,17},{2,10},{10... | collective-permute-start | bytes 3145736 | tf_op jit(solution)/shard_map/ppermute | solution.py:72
  339.0 283.0 %reduce-scatter.5.cloned.1.call-start = ((), (), s32[]{:S(2)}) async-start(), calls=%async_computation.12 | async-start | bytes 1769472 | tf_op jit(solution)/shard_map/reduce_scatter | solution.py:211
  427.0 203.5 %reduce-scatter.9.cloned.1.call-start = ((), (), s32[]{:S(2)}) async-start(), calls=%async_computation.14 | async-start | bytes 9437184 | tf_op jit(solution)/shard_map/reduce_scatter | solution.py:211
  450.7 185.2 %reduce-scatter.7.cloned.1.call-start = ((), (), s32[]{:S(2)}) async-start(), calls=%async_computation.13 | async-start | bytes 1179648 | tf_op jit(solution)/shard_map/reduce_scatter | solution.py:231
  452.3 24.2 %collective-permute-start.30 = (bf16[256,2048]{1,0:T(8,128)(2,1)}, bf16[256,2048]{1,0:T(8,128)(2,1)S(1)}, u32[]{:S(2)}, u32[]{:S(2)}) collective-permute-start(bf16[256,2048]{1,0:T(8,128)(2,1)} %get-tuple-element.22), channel_id=1, source_target_pairs={{0,8},{8,0},{16,24},{24,16},{1,9},{9,1},{17,25},{25,17},{2,10},{10... | collective-permute-start | bytes 3145736 | tf_op jit(solution)/shard_map/ppermute | solution.py:72
  491.4 149.3 %reduce-scatter.11.cloned.1.call-start = ((), (), s32[]{:S(2)}) async-start(), calls=%async_computation.15 | async-start | bytes 4718592 | tf_op jit(solution)/shard_map/reduce_scatter | solution.py:202
  502.9 30.9 %collective-permute-start.27 = (bf16[2048,384]{1,0:T(8,128)(2,1)}, bf16[2048,384]{1,0:T(8,128)(2,1)}, u32[]{:S(2)}, u32[]{:S(2)}) collective-permute-start(bf16[2048,384]{1,0:T(8,128)(2,1)} %slice.188), channel_id=1, source_target_pairs={{0,16},{8,24},{16,0},{24,8},{1,17},{9,25},{17,1},{25,9},{2,18},{10... | collective-permute-start | bytes 4718600 | tf_op jit(solution)/shard_map/ppermute | solution.py:72
  503.0 33.0 %collective-permute-start.26 = (bf16[2048,384]{1,0:T(8,128)(2,1)}, bf16[2048,384]{1,0:T(8,128)(2,1)}, u32[]{:S(2)}, u32[]{:S(2)}) collective-permute-start(bf16[2048,384]{1,0:T(8,128)(2,1)} %slice.188), channel_id=1, source_target_pairs={{0,8},{8,0},{16,24},{24,16},{1,9},{9,1},{17,25},{25,17},{2,10},{10... | collective-permute-start | bytes 4718600 | tf_op jit(solution)/shard_map/ppermute | solution.py:72
  (77 other events, 1689.5 us)
Sparse Core Ops, SparseCore 0:
  10.2 43.0 all-gather.6
  55.5 30.0 all-gather.4
  87.8 81.5 all-gather.8
  170.8 45.6 all-gather.10
  427.1 39.8 reduce-scatter.4
  469.2 87.3 reduce-scatter.8
  559.5 30.7 reduce-scatter.6
  592.5 48.1 reduce-scatter.10
